TPU v7x, 32 devices: a whole 2x2x4 slice. The times are simulated.
32 devices in a mesh: lon: 8 (over y, x, core), spec: 4 (over z).
Axes of the slice: x: 2, y: 2, z: 4, core: 2. Of those that a mesh axis runs over, the one named last changes fastest.
Arguments:
- lam_final: float32 [1296, 64, 1024], P('spec', None, 'lon'), may hold values from -6 to 6
- stored_source: bfloat16 [2, 1296, 64, 1024], P(None, 'spec', None, 'lon'), may hold values from 0.19921875 to 1.1953125
- mixing: bfloat16 [1296, 1296], replicated, may hold values from -0.15625 to 0.15625
- drift_x: float32 [1296], replicated, may hold values from -0.45 to 0.45
- drift_y: float32 [1296], replicated, may hold values from -0.45 to 0.45
- ocean_mask: int32 [64, 1024], P(None, 'lon'), may hold values 0 or 1
- misfit: float32 [2, 64, 1024], P(None, None, 'lon'), may hold values from -6 to 6
- obs_mask: int32 [2, 64, 1024], P(None, None, 'lon'), may hold values 0 or 1
Outputs:
- lam_start: float32 [1296, 64, 1024], P('spec', None, 'lon')
All inputs are finite; a program needn't handle non-finite values. No bound on the sum of `ocean_mask` or of `obs_mask` on one device may be relied on, other than what follows from the above.
Results may differ from a plain program's by a relative error of at most 0.0028.
Values may be sent and summed in bfloat16 or wider, within the bound.
A program may use at most 192 MiB of HBM per device.

v0:
```python
import jax
import jax.numpy as jnp
from jax import lax
from jax.sharding import PartitionSpec as P

STEPS = 2


def with_halo(block, sides, width):
    for axis, dim in sides:
        count = lax.axis_size(axis)
        forward = [(i, i + 1) for i in range(count - 1)]
        forward.append((count - 1, 0))
        backward = [(target, source) for source, target in forward]
        low = lax.ppermute(
            lax.slice_in_dim(block, block.shape[dim] - width, None, axis=dim), axis, forward
        )
        high = lax.ppermute(lax.slice_in_dim(block, 0, width, axis=dim), axis, backward)
        block = jnp.concatenate([low, block, high], axis=dim)
    return block


def couple_local(rounded, mixing):
    flat = rounded.reshape(rounded.shape[0], -1)
    coupled = lax.dot_general(
        mixing, flat, (((0,), (0,)), ((), ())), preferred_element_type=jnp.float32
    )
    return coupled.astype(jnp.bfloat16).reshape(rounded.shape)


def advect_step(adjoint, speed_x, speed_y, northern, southern):
    padded = with_halo(adjoint, (("lon", 2),), 1)
    eastern = padded[:, :, 2:]
    western = padded[:, :, :-2]
    speed_x = speed_x[:, None, None]
    speed_y = speed_y[:, None, None]
    stay = 1.0 - jnp.abs(speed_x) - jnp.abs(speed_y)
    result = (
        stay * adjoint + jnp.maximum(speed_x, 0.0) * eastern + jnp.maximum(-speed_x, 0.0) * western
    )
    return result + jnp.maximum(speed_y, 0.0) * northern + jnp.maximum(-speed_y, 0.0) * southern


def per_device(lam_final, stored_source, mixing, drift_x, drift_y, ocean_mask, misfit, obs_mask):
    spec_index = lax.axis_index("spec")
    own_count = lam_final.shape[0]
    speed_x = lax.dynamic_slice_in_dim(drift_x, spec_index * own_count, own_count)
    speed_y = lax.dynamic_slice_in_dim(drift_y, spec_index * own_count, own_count)
    ocean_field = ocean_mask.astype(jnp.float32)[None]
    adjoint = lam_final
    for step_index in reversed(range(STEPS)):
        forcing = misfit[step_index] * obs_mask[step_index].astype(jnp.float32)
        adjoint = (adjoint + forcing[None]) * ocean_field
        rounded = adjoint.astype(jnp.bfloat16)
        coupled = couple_local(
            lax.all_to_all(rounded, "spec", split_axis=1, concat_axis=0, tiled=True), mixing
        )
        coupled = lax.all_to_all(coupled, "spec", split_axis=0, concat_axis=1, tiled=True)
        adjoint = adjoint + stored_source[step_index].astype(jnp.float32) * coupled.astype(
            jnp.float32
        )
        zero_row = jnp.zeros_like(adjoint[:, :1])
        northern = jnp.concatenate([adjoint[:, 1:], zero_row], axis=1)
        southern = jnp.concatenate([zero_row, adjoint[:, :-1]], axis=1)
        adjoint = advect_step(adjoint, speed_x, speed_y, northern, southern)
    return adjoint


def solution(mesh):
    in_specs = (
        P("spec", None, "lon"),
        P(None, "spec", None, "lon"),
        P(),
        P(),
        P(),
        P(None, "lon"),
        P(None, None, "lon"),
        P(None, None, "lon"),
    )
    out_specs = P("spec", None, "lon")
    return jax.shard_map(
        per_device, mesh=mesh, in_specs=in_specs, out_specs=out_specs, check_vma=False
    )
```

profile of v0, /device:TPU:8, one launch (start us, length us, event | category | flops | bytes accessed | tf_op | source)
XLA Modules:
  0.0 731.6 jit_solution(17673067778883216311)
XLA Ops:
  0.0 0.8 convert_element_type.66
  0.8 0.8 multiply_bitcast_fusion.1
  1.6 11.5 %fusion.17 = bf16[324,64,128]{2,0,1:T(8,128)(2,1)S(1)} fusion(f32[324,64,128]{2,1,0:T(8,128)} %param.8, f32[64,128]{1,0:T(8,128)S(1)} %convert_element_type.66, f32[64,128]{1,0:T(8,128)S(1)} %get-tuple-element.17), kind=kLoop, calls=%fused_computation.24 | loop fusion | flops 7962624 | bytes 15990784 | tf_op jit(solution)/shard_map/convert_element_type | solution.py:54
  13.1 0.0 copy-start.2
  13.1 122.5 %all_to_all.48 = bf16[324,64,128]{2,0,1:T(8,128)(2,1)S(1)} all-to-all(bf16[324,64,128]{2,0,1:T(8,128)(2,1)S(1)} %fusion.17), channel_id=1, replica_groups=mesh['lon'=8,'spec'=4] {'spec'}, dimensions={1} | all-to-all | bytes 10616832 | tf_op jit(solution)/shard_map/all_to_all | solution.py:56
  135.6 0.8 copy.17
  136.4 0.0 copy-done.2
  136.4 9.2 %fusion.22 = bf16[162,8,16,128]{3,1,2,0:T(8,128)(2,1)S(1)} fusion(bf16[1296,1296]{1,0:T(8,128)(2,1)S(1)} %copy-done.2, bf16[162,8,16,128]{3,2,1,0:T(8,128)(2,1)S(1)} %bitcast.67), kind=kOutput, calls=%fused_computation.33 | convolution fusion | flops 6882361344 | bytes 13976064 | tf_op jit(solution)/shard_map/dot_general | solution.py:25
  145.6 4.2 copy.34
  149.8 7.0 all-to-all-start.1
  156.8 0.8 abs_subtract_fusion
  157.6 10.6 %fusion.34 = (bf16[1,324,64,128]{3,2,1,0:T(8,128)(2,1)}, bf16[1,324,64,128]{3,2,1,0:T(8,128)(2,1)}) fusion(bf16[2,324,64,128]{3,2,1,0:T(8,128)(2,1)} %param.9), kind=kLoop, calls=%fused_computation.47 | loop fusion | bytes 21233664 | tf_op jit(solution)/shard_map/slice | solution.py:59
  168.2 0.0 slice-start.3
  168.2 101.4 %all-to-all-done.1 = bf16[1296,16,128]{2,1,0:T(8,128)(2,1)} async-done(((bf16[1296,16,128]{2,1,0:T(8,128)(2,1)}), bf16[1296,16,128]{2,1,0:T(8,128)(2,1)}, u32[]{:S(2)}, u32[]{:S(2)}) %all-to-all-start.1) | async-done | bytes 5308448 | tf_op jit(solution)/shard_map/all_to_all | solution.py:58
  269.7 0.0 slice-start.4
  269.7 3.7 copy.18
  273.4 0.0 slice-done.3
  273.4 0.1 slice-done.4
  273.5 12.9 %fusion.15 = f32[324,64,128]{2,0,1:T(8,128)S(1)} fusion(f32[4,324,16,128]{3,1,2,0:T(8,128)S(1)} %copy.18, f32[324,64,128]{2,1,0:T(8,128)} %param.8, bf16[1,324,64,128]{3,2,1,0:T(8,128)(2,1)S(1)} %bitcast.63, f32[64,128]{1,0:T(8,128)S(1)} %convert_element_type.66, f32[64,128]{1,0:T(8,128)S(1)} %get-tuple-element.17), kind=kLoop, calls=%fused_computation.21 | loop fusion | flops 13271040 | bytes 37224448 | tf_op jit(solution)/shard_map/add | solution.py:59
  286.4 0.0 copy-start
  286.4 9.5 %fusion.32 = (f32[324,64,1]{2,0,1:T(8,128)}, f32[324,64,1]{2,0,1:T(8,128)}) fusion(f32[324,64,128]{2,0,1:T(8,128)S(1)} %fusion.15), kind=kLoop, calls=%fused_computation.45 | loop fusion | bytes 331776 | tf_op jit(solution)/shard_map/slice | solution.py:18
  295.9 1.0 copy-done
  296.9 6.5 copy.19
  303.4 6.5 copy.21
  309.9 0.1 collective-permute-start.1
  310.0 2.8 collective-permute-start
  312.8 15.7 %fusion.33 = (f32[324,63,128]{2,0,1:T(8,128)}, f32[324,63,128]{2,0,1:T(8,128)}) fusion(f32[324,64,128]{2,0,1:T(8,128)} %copy-done), kind=kLoop, calls=%fused_computation.46 | loop fusion | bytes 41803776 | tf_op jit(solution)/shard_map/slice | solution.py:63
  328.5 0.0 collective-permute-done
  328.5 5.6 copy.20
  334.1 0.0 collective-permute-done.1
  334.1 5.6 copy.22
  339.7 30.8 %fusion.28 = (bf16[324,64,128]{2,0,1:T(8,128)(2,1)S(1)}, f32[324,64,128]{2,0,1:T(8,128)}) fusion(f32[64,128]{1,0:T(8,128)S(1)} %convert_element_type.66, f32[64,128]{1,0:T(8,128)S(1)} %get-tuple-element.18, f32[324,63,128]{2,0,1:T(8,128)} %get-tuple-element.14, f32[324]{0:T(512)S(1)} %get-tuple-element.23, f32[324,63,128]{2,0,1:T(8,128)} %get-tuple-element.13, ...), kind=kLoop, calls=%fused_computation.42 | loop fusion | flops 37158912 | bytes 47681872 | tf_op jit(solution)/shard_map/convert_element_type | solution.py:54
  370.5 0.0 copy-start.3
  370.5 122.6 %all_to_all.49 = bf16[324,64,128]{2,0,1:T(8,128)(2,1)S(1)} all-to-all(bf16[324,64,128]{2,0,1:T(8,128)(2,1)S(1)} %get-tuple-element.5), channel_id=1, replica_groups=mesh['lon'=8,'spec'=4] {'spec'}, dimensions={1} | all-to-all | bytes 10616832 | tf_op jit(solution)/shard_map/all_to_all | solution.py:56
  493.1 0.8 copy.24
  493.8 0.0 copy-done.3
  493.9 9.5 %fusion.25 = bf16[162,8,16,128]{3,1,2,0:T(8,128)(2,1)S(1)} fusion(bf16[1296,1296]{1,0:T(8,128)(2,1)S(1)} %copy-done.3, bf16[162,8,16,128]{3,2,1,0:T(8,128)(2,1)S(1)} %bitcast.68), kind=kOutput, calls=%fused_computation.34 | convolution fusion | flops 6882361344 | bytes 13976064 | tf_op jit(solution)/shard_map/dot_general | solution.py:25
  503.3 1.8 copy.36
  505.2 0.0 slice-start
  505.2 0.0 slice-start.1
  505.2 119.5 %all_to_all.50 = bf16[1296,16,128]{2,1,0:T(8,128)(2,1)S(1)} all-to-all(bf16[1296,16,128]{2,1,0:T(8,128)(2,1)S(1)} %bitcast.65), channel_id=1, replica_groups=mesh['lon'=8,'spec'=4] {'spec'}, dimensions={0} | all-to-all | bytes 10616832 | tf_op jit(solution)/shard_map/all_to_all | solution.py:58
  624.7 0.0 slice-start.2
  624.7 5.0 copy.25
  629.6 0.0 slice-done
  629.6 0.0 slice-done.1
  629.6 0.0 slice-done.2
  629.7 8.3 %fusion.14 = f32[324,64,128]{2,0,1:T(8,128)S(1)} fusion(f32[324,64,128]{2,0,1:T(8,128)S(1)} %bitcast.59, f32[4,324,16,128]{3,1,2,0:T(8,128)} %copy.25, bf16[1,324,64,128]{3,2,1,0:T(8,128)(2,1)} %get-tuple-element.15), kind=kLoop, calls=%fused_computation.19 | loop fusion | flops 7962624 | bytes 37158912 | tf_op jit(solution)/shard_map/add | solution.py:59
  638.0 0.0 copy-start.1
  638.0 9.4 %fusion.31 = (f32[324,64,1]{2,0,1:T(8,128)}, f32[324,64,1]{2,0,1:T(8,128)}) fusion(f32[324,64,128]{2,0,1:T(8,128)S(1)} %fusion.14), kind=kLoop, calls=%fused_computation.44 | loop fusion | bytes 331776 | tf_op jit(solution)/shard_map/slice | solution.py:18
  647.4 1.1 copy-done.1
  648.4 6.5 copy.26
  654.9 6.5 copy.28
  661.4 0.1 collective-permute-start.3
  661.5 2.6 collective-permute-start.2
  664.1 15.7 %fusion.30 = (f32[324,63,128]{2,0,1:T(8,128)}, f32[324,63,128]{2,0,1:T(8,128)}) fusion(f32[324,64,128]{2,0,1:T(8,128)} %copy-done.1), kind=kLoop, calls=%fused_computation.43 | loop fusion | bytes 41803776 | tf_op jit(solution)/shard_map/slice | solution.py:63
  679.8 0.0 collective-permute-done.2
  679.8 5.6 copy.27
  685.3 0.0 collective-permute-done.3
  685.3 5.6 copy.29
  691.0 29.9 %fusion.3 = f32[324,64,128]{2,0,1:T(8,128)} fusion(f32[324,64,128]{2,0,1:T(8,128)} %copy-done.1, f32[324,64,1]{2,0,1:T(8,128)} %copy.29, f32[324,64,1]{2,0,1:T(8,128)} %copy.27, f32[324,63,128]{2,0,1:T(8,128)} %get-tuple-element.8, f32[324,63,128]{2,0,1:T(8,128)} %get-tuple-element.7, f32[324]{0:T(512)S(1)} %get-tuple-element.23, ...), kind=kLoop, calls=%fused_computation.4 | loop fusion | flops 29196288 | bytes 42307920 | tf_op jit(solution)/shard_map/add | solution.py:41
  720.9 10.2 %copy.30 = f32[324,64,128]{2,1,0:T(8,128)} copy(f32[324,64,128]{2,0,1:T(8,128)} %fusion.3) | data formatting | bytes 21233664 | tf_op jit(solution)/shard_map/add | solution.py:41
  (2 shorter events, 0.0 us)
Async XLA Ops:
  13.1 123.2 %copy-start.2 = (bf16[1296,1296]{1,0:T(8,128)(2,1)S(1)}, bf16[1296,1296]{1,0:T(8,128)(2,1)}, u32[]{:S(2)}) copy-start(bf16[1296,1296]{1,0:T(8,128)(2,1)} %param.10) | copy-start | bytes 10077700
  149.8 119.9 %all-to-all-start.1 = ((bf16[1296,16,128]{2,1,0:T(8,128)(2,1)}), bf16[1296,16,128]{2,1,0:T(8,128)(2,1)}, u32[]{:S(2)}, u32[]{:S(2)}) async-start(bf16[1296,16,128]{2,1,0:T(8,128)(2,1)} %bitcast.64), calls=%async_computation.1 | async-start | bytes 10616832 | tf_op jit(solution)/shard_map/all_to_all | solution.py:58
  168.2 105.1 %slice-start.3 = ((s8[5308416]{0:T(1024)(128)(4,1)}), s8[1114112]{0:T(1024)(128)(4,1)S(1)}, s32[]{:S(2)}) async-start(s8[5308416]{0:T(1024)(128)(4,1)} %bitcast.62), calls=%async_computation.7 | async-start | bytes 2228224
  269.7 3.8 slice-start.4
  286.4 10.6 %copy-start = (f32[324,64,128]{2,0,1:T(8,128)}, f32[324,64,128]{2,0,1:T(8,128)S(1)}, u32[]{:S(2)}) copy-start(f32[324,64,128]{2,0,1:T(8,128)S(1)} %fusion.15) | copy-start | bytes 31850500
  309.9 24.2 %collective-permute-start.1 = (f32[324,64,1]{0,1,2:T(8,128)S(1)}, f32[324,64,1]{0,1,2:T(8,128)S(1)}, u32[]{:S(2)}, u32[]{:S(2)}) collective-permute-start(f32[324,64,1]{0,1,2:T(8,128)S(1)} %copy.21), channel_id=1, source_target_pairs={{0,4},{4,8},{8,12},{12,16},{16,20},{20,24},{24,28},{28,0},{1,5},{5... | collective-permute-start | bytes 248840 | tf_op jit(solution)/shard_map/ppermute | solution.py:15
  310.0 18.5 %collective-permute-start = (f32[324,64,1]{0,1,2:T(8,128)S(1)}, f32[324,64,1]{0,1,2:T(8,128)S(1)}, u32[]{:S(2)}, u32[]{:S(2)}) collective-permute-start(f32[324,64,1]{0,1,2:T(8,128)S(1)} %copy.19), channel_id=1, source_target_pairs={{4,0},{8,4},{12,8},{16,12},{20,16},{24,20},{28,24},{0,28},{5,1},{9... | collective-permute-start | bytes 248840 | tf_op jit(solution)/shard_map/ppermute | solution.py:18
  370.5 123.4 %copy-start.3 = (bf16[1296,1296]{1,0:T(8,128)(2,1)S(1)}, bf16[1296,1296]{1,0:T(8,128)(2,1)}, u32[]{:S(2)}) copy-start(bf16[1296,1296]{1,0:T(8,128)(2,1)} %param.10) | copy-start | bytes 10077700
  505.2 124.5 %slice-start = ((s8[10747904]{0:T(1024)(128)(4,1)}), s8[4194304]{0:T(1024)(128)(4,1)S(1)}, s32[]{:S(2)}) async-start(s8[10747904]{0:T(1024)(128)(4,1)} %bitcast.58), calls=%async_computation.4 | async-start | bytes 8388608
  505.2 124.5 %slice-start.1 = ((s8[10747904]{0:T(1024)(128)(4,1)}), s8[4194304]{0:T(1024)(128)(4,1)S(1)}, s32[]{:S(2)}) async-start(s8[10747904]{0:T(1024)(128)(4,1)} %bitcast.58), calls=%async_computation.5 | async-start | bytes 8388608
  624.7 5.0 slice-start.2
  638.0 10.4 %copy-start.1 = (f32[324,64,128]{2,0,1:T(8,128)}, f32[324,64,128]{2,0,1:T(8,128)S(1)}, u32[]{:S(2)}) copy-start(f32[324,64,128]{2,0,1:T(8,128)S(1)} %fusion.14) | copy-start | bytes 31850500
  661.4 23.9 %collective-permute-start.3 = (f32[324,64,1]{0,1,2:T(8,128)S(1)}, f32[324,64,1]{0,1,2:T(8,128)S(1)}, u32[]{:S(2)}, u32[]{:S(2)}) collective-permute-start(f32[324,64,1]{0,1,2:T(8,128)S(1)} %copy.28), channel_id=1, source_target_pairs={{0,4},{4,8},{8,12},{12,16},{16,20},{20,24},{24,28},{28,0},{1,5},{5... | collective-permute-start | bytes 248840 | tf_op jit(solution)/shard_map/ppermute | solution.py:15
  661.5 18.3 %collective-permute-start.2 = (f32[324,64,1]{0,1,2:T(8,128)S(1)}, f32[324,64,1]{0,1,2:T(8,128)S(1)}, u32[]{:S(2)}, u32[]{:S(2)}) collective-permute-start(f32[324,64,1]{0,1,2:T(8,128)S(1)} %copy.26), channel_id=1, source_target_pairs={{4,0},{8,4},{12,8},{16,12},{20,16},{24,20},{28,24},{0,28},{5,1},{9... | collective-permute-start | bytes 248840 | tf_op jit(solution)/shard_map/ppermute | solution.py:18
where the time goes:
time: 741 us; the launch traced here: 732 us
  blocking collectives  365 us (49%)
  local copies, waits for them, and re-layouts  138 us (19%)
  waiting for transfers between devices  101 us (14%)
  other arithmetic  95.9 us (13%)
  matrix products  18.7 us (3%)
  starting transfers between devices  12.6 us (2%)
    all_to_all x2, blocking collectives, per_device(): lax.all_to_all(rounded, 'spec', split_axis=1, concat_axis=0, tiled=True)  245 us
    all_to_all x1, blocking collectives, per_device(): lax.all_to_all(coupled, 'spec', split_axis=0, concat_axis=1, tiled=True)  119 us
    all_to_all x1, waiting for transfers between devices, per_device(): lax.all_to_all(coupled, 'spec', split_axis=0, concat_axis=1, tiled=True)  101 us
    convert_element_type x2, other arithmetic, per_device(): rounded = adjoint.astype(jnp.bfloat16)  42.3 us
    slice x4, local copies, waits for them, and re-layouts, with_halo(): lax.slice_in_dim(block, 0, width, axis=dim)  31.8 us
    slice x2, local copies, waits for them, and re-layouts, per_device(): northern = jnp.concatenate([adjoint[:, 1:], zero_row], axis=1)  31.4 us
    add x1, other arithmetic, advect_step(): result + jnp.maximum(speed_y, 0.0) * northern  29.9 us
    add x2, other arithmetic, per_device(): adjoint + stored_source[step_index].astype(jnp.float32) * coupled.astype(...  21.3 us
  transfers between devices with their start and end apart: 5, of which 1 were waited for; matrix products, arithmetic and copies ran while one was open for 7% of the time, Pallas kernels for 0%

commit v1 on v0

v1 whole, which is shorter than its diff:
```python
import functools

import jax
import jax.numpy as jnp
from jax import lax
from jax.experimental import pallas as pl
from jax.experimental.pallas import tpu as pltpu
from jax.sharding import PartitionSpec as P

CHUNKS = 4
MESH = pl.DeviceIdType.MESH


def chunk_bounds(own):
    inner = [int(round(own * q / CHUNKS / 16)) * 16 for q in range(1, CHUNKS)]
    edges = [0] + inner + [own]
    return list(zip(edges[:-1], edges[1:]))


def round_up(value, unit):
    return -(-value // unit) * unit


def group_of(count):
    return 4 if count % 4 == 0 else (2 if count % 2 == 0 else 1)


def kernel(
    steps, parts, ring, bounds, own_pad,
    lam, source, weights, drift_x, drift_y, ocean_mask, misfit, obs_mask,
    out,
    state, send_in, recv_in, send_out, recv_out, flat, weight_buf, spread, unpack,
    source_buf, halo_send, halo_recv,
    send_sem, recv_sem, halo_send_sem, halo_recv_sem, lam_sem, source_sem, weight_sem, out_sem,
):
    me = lax.axis_index("spec")
    lon = lax.axis_index("lon")
    own, lat, width = state.shape
    rows = lat // parts
    east, west = lax.rem(lon + 1, ring), lax.rem(lon + ring - 1, ring)
    chunks = len(bounds)
    peers = list(range(1, parts))
    order = [(step, q) for step in reversed(range(steps)) for q in range(chunks)]

    def peer(offset):
        return lax.rem(me + offset, parts)

    def lam_copy(q):
        low, high = bounds[q]
        return pltpu.make_async_copy(
            lam.at[pl.ds(low, high - low)], state.at[pl.ds(low, high - low)], lam_sem.at[q]
        )

    def source_copy(position):
        step, q = order[position]
        low, high = bounds[q]
        slot = position % 2
        return pltpu.make_async_copy(
            source.at[step, pl.ds(low, high - low)],
            source_buf.at[slot, pl.ds(0, high - low)],
            source_sem.at[slot],
        )

    def out_copy(q):
        low, high = bounds[q]
        return pltpu.make_async_copy(
            state.at[pl.ds(low, high - low)], out.at[pl.ds(low, high - low)], out_sem.at[q]
        )

    weight_copy = pltpu.make_async_copy(weights, weight_buf, weight_sem)

    def exchange(phase, q, offset):
        low, high = bounds[q]
        sender, receiver = (send_in, recv_in) if phase == 0 else (send_out, recv_out)
        target = peer(offset)
        return pltpu.make_async_remote_copy(
            src_ref=sender.at[target, pl.ds(low, high - low)],
            dst_ref=receiver.at[me, pl.ds(low, high - low)],
            send_sem=send_sem.at[phase, q, offset - 1],
            recv_sem=recv_sem.at[phase, q, me],
            device_id={"spec": target},
            device_id_type=MESH,
        )

    def arrival(phase, q, offset):
        low, high = bounds[q]
        sender, receiver = (send_in, recv_in) if phase == 0 else (send_out, recv_out)
        origin = peer(offset)
        return pltpu.make_async_remote_copy(
            src_ref=sender.at[origin, pl.ds(low, high - low)],
            dst_ref=receiver.at[origin, pl.ds(low, high - low)],
            send_sem=send_sem.at[phase, q, offset - 1],
            recv_sem=recv_sem.at[phase, q, origin],
            device_id={"spec": origin},
            device_id_type=MESH,
        )

    def halo(position, side):
        return pltpu.make_async_remote_copy(
            src_ref=halo_send.at[position, side],
            dst_ref=halo_recv.at[position, side],
            send_sem=halo_send_sem.at[position, side],
            recv_sem=halo_recv_sem.at[position, side],
            device_id={"lon": west if side == 0 else east},
            device_id_type=MESH,
        )

    for q in range(chunks):
        lam_copy(q).start()
    weight_copy.start()
    source_copy(0).start()
    source_copy(1).start()

    barrier = pltpu.get_barrier_semaphore()
    for offset in peers:
        pl.semaphore_signal(barrier, inc=1, device_id={"spec": peer(offset)}, device_id_type=MESH)
    for side in (west, east):
        pl.semaphore_signal(barrier, inc=1, device_id={"lon": side}, device_id_type=MESH)
    pl.semaphore_wait(barrier, len(peers) + 2)

    ocean = ocean_mask[...].astype(jnp.float32)
    row = lax.broadcasted_iota(jnp.int32, (lat, width), 0)
    lane = lax.broadcasted_iota(jnp.int32, (lat, width), 1)

    def forcing_of(step):
        return misfit[step] * obs_mask[step].astype(jnp.float32)

    def emit(adjoint, c):
        state[c] = adjoint
        rounded = adjoint.astype(jnp.bfloat16)
        for part in range(parts):
            send_in[part, c] = rounded[part * rows : (part + 1) * rows]

    forcing = forcing_of(steps - 1)
    for q in range(chunks):
        low, high = bounds[q]
        lam_copy(q).wait()

        def prepare(c, carry):
            emit((state[c] + forcing) * ocean, c)
            return carry

        lax.fori_loop(low, high, prepare, 0)
        for offset in peers:
            exchange(0, q, offset).start()

    for step in reversed(range(steps)):
        last = step == 0

        for q in range(chunks):
            low, high = bounds[q]
            count = high - low
            padded = round_up(count, 16)
            group = group_of(count)

            for offset in range(parts):
                origin = peer(offset)
                if offset:
                    arrival(0, q, offset).wait_recv()
                block = recv_in if offset else send_in
                if padded != count:
                    unpack[pl.ds(count * rows, (padded - count) * rows)] = jnp.zeros(
                        ((padded - count) * rows, width), jnp.float32
                    )

                def widen(t, carry):
                    value = block[origin, pl.ds(low + t * group, group)]
                    unpack[pl.ds(pl.multiple_of(t * group * rows, 8), group * rows)] = value.astype(
                        jnp.float32
                    ).reshape(group * rows, width)
                    return carry

                lax.fori_loop(0, count // group, widen, 0)
                base = pl.multiple_of(origin * own_pad + low, 16)
                for i in range(rows):
                    flat[pl.ds(base, padded), pl.ds(i * width, width)] = unpack[
                        pl.ds(i, padded, stride=rows)
                    ].astype(jnp.bfloat16)

        if step == steps - 1:
            weight_copy.wait()
        start = 0
        for q in range(chunks):
            low, high = bounds[q]
            count = high - low
            tall = round_up(count, 8)
            group = group_of(count)
            total = parts * tall

            def multiply(pair, carry):
                columns = pl.ds(pl.multiple_of(pair * 2 * width, 2 * width), 2 * width)
                result = jnp.dot(
                    weight_buf[start : start + total],
                    flat[:, columns],
                    preferred_element_type=jnp.float32,
                )
                spread[pl.ds(pair * 2, total, stride=rows)] = result[:, :width]
                spread[pl.ds(pair * 2 + 1, total, stride=rows)] = result[:, width:]
                return carry

            lax.fori_loop(0, rows // 2, multiply, 0)
            if not step == steps - 1:
                for offset in peers:
                    exchange(1, q, offset).wait_send()
            for part in range(parts):

                def narrow(t, carry):
                    place = pl.multiple_of((part * tall + t * group) * rows, 8)
                    value = spread[pl.ds(place, group * rows)]
                    send_out[part, pl.ds(low + t * group, group)] = value.reshape(
                        group, rows, width
                    ).astype(jnp.bfloat16)
                    return carry

                lax.fori_loop(0, count // group, narrow, 0)
            for offset in peers:
                exchange(1, q, offset).start()
            recv_out[me, pl.ds(low, count)] = send_out[me, pl.ds(low, count)]
            start += total

        forcing = None if last else forcing_of(step - 1)
        for q in range(chunks):
            low, high = bounds[q]
            count = high - low
            position = (steps - 1 - step) * chunks + q
            slot = position % 2
            source_copy(position).wait()
            for offset in peers:
                arrival(1, q, offset).wait_recv()

            def update(c, carry):
                to_west, to_east = carry
                coupled = jnp.concatenate(
                    [recv_out[part, c].astype(jnp.float32) for part in range(parts)], axis=0
                )
                factor = source_buf[slot, c - low].astype(jnp.float32)
                adjoint = state[c] + factor * coupled
                state[c] = adjoint
                to_west = jnp.where(lane == 0, adjoint, pltpu.roll(to_west, 1, 1))
                to_east = jnp.where(lane == width - 1, adjoint, pltpu.roll(to_east, width - 1, 1))
                return to_west, to_east

            zero = jnp.zeros((lat, width), jnp.float32)
            to_west, to_east = lax.fori_loop(low, high, update, (zero, zero))
            halo_send[position, 0] = to_west
            halo_send[position, 1] = to_east
            halo(position, 0).start()
            halo(position, 1).start()
            if position + 2 < len(order):
                source_copy(position + 2).start()
            if not last:
                for offset in peers:
                    exchange(0, q, offset).wait_send()
            halo(position, 0).wait()
            halo(position, 1).wait()

            def advect(c, carry):
                from_east, from_west = carry
                adjoint = state[c]
                speed_x = drift_x[me * own + c]
                speed_y = drift_y[me * own + c]
                eastern = jnp.where(lane == width - 1, from_east, pltpu.roll(adjoint, width - 1, 1))
                western = jnp.where(lane == 0, from_west, pltpu.roll(adjoint, 1, 1))
                northern = jnp.where(row == lat - 1, 0.0, pltpu.roll(adjoint, lat - 1, 0))
                southern = jnp.where(row == 0, 0.0, pltpu.roll(adjoint, 1, 0))
                stay = 1.0 - jnp.abs(speed_x) - jnp.abs(speed_y)
                result = (
                    stay * adjoint
                    + jnp.maximum(speed_x, 0.0) * eastern
                    + jnp.maximum(-speed_x, 0.0) * western
                )
                result = (
                    result
                    + jnp.maximum(speed_y, 0.0) * northern
                    + jnp.maximum(-speed_y, 0.0) * southern
                )
                if last:
                    state[c] = result
                else:
                    emit((result + forcing) * ocean, c)
                return pltpu.roll(from_east, 1, 1), pltpu.roll(from_west, width - 1, 1)

            from_east = pltpu.roll(halo_recv[position, 0], (width - count) % width, 1)
            from_west = pltpu.roll(halo_recv[position, 1], count % width, 1)
            lax.fori_loop(low, high, advect, (from_east, from_west))
            if last:
                out_copy(q).start()
            else:
                for offset in peers:
                    exchange(0, q, offset).start()

    for q in range(chunks):
        for offset in peers:
            exchange(0, q, offset).wait_send()
            exchange(1, q, offset).wait_send()
        out_copy(q).wait()


def arrange_weights(mixing, parts, own, own_pad, bounds):
    table = mixing.T.reshape(parts, own, parts, own)
    table = jnp.pad(table, ((0, 0), (0, 0), (0, 0), (0, own_pad - own)))
    pieces = []
    for low, high in bounds:
        tall = round_up(high - low, 8)
        piece = jnp.pad(table[:, low:high], ((0, 0), (0, tall - (high - low)), (0, 0), (0, 0)))
        pieces.append(piece.reshape(parts * tall, parts * own_pad))
    return jnp.concatenate(pieces, axis=0)


def per_device(
    parts, ring, lam_final, stored_source, mixing, drift_x, drift_y, ocean_mask, misfit, obs_mask
):
    steps = stored_source.shape[0]
    own, lat, width = lam_final.shape
    rows = lat // parts
    bounds = chunk_bounds(own)
    own_pad = round_up(own, 16)
    largest = max(high - low for low, high in bounds)
    weights = arrange_weights(mixing, parts, own, own_pad, bounds)
    vmem = pl.BlockSpec(memory_space=pltpu.VMEM)
    smem = pl.BlockSpec(memory_space=pltpu.SMEM)
    hbm = pl.BlockSpec(memory_space=pl.ANY)
    block = pltpu.VMEM((parts, own, rows, width), jnp.bfloat16)
    dma = pltpu.SemaphoreType.DMA
    positions = steps * CHUNKS
    return pl.pallas_call(
        functools.partial(kernel, steps, parts, ring, bounds, own_pad),
        out_shape=jax.ShapeDtypeStruct(lam_final.shape, jnp.float32),
        in_specs=[hbm, hbm, hbm, smem, smem, vmem, vmem, vmem],
        out_specs=hbm,
        scratch_shapes=[
            pltpu.VMEM((own, lat, width), jnp.float32),
            block, block, block, block,
            pltpu.VMEM((parts * own_pad, rows * width), jnp.bfloat16),
            pltpu.VMEM(weights.shape, jnp.bfloat16),
            pltpu.VMEM((parts * round_up(largest, 8) * rows, width), jnp.float32),
            pltpu.VMEM((round_up(largest, 16) * rows, width), jnp.float32),
            pltpu.VMEM((2, largest, lat, width), jnp.bfloat16),
            pltpu.VMEM((positions, 2, lat, width), jnp.float32),
            pltpu.VMEM((positions, 2, lat, width), jnp.float32),
            dma((2, CHUNKS, parts - 1)),
            dma((2, CHUNKS, parts)),
            dma((positions, 2)),
            dma((positions, 2)),
            dma((CHUNKS,)),
            dma((2,)),
            dma,
            dma((CHUNKS,)),
        ],
        compiler_params=pltpu.CompilerParams(
            collective_id=0, has_side_effects=True, vmem_limit_bytes=60 * 1024 * 1024
        ),
    )(lam_final, stored_source, weights, drift_x, drift_y, ocean_mask, misfit, obs_mask)


def solution(mesh):
    in_specs = (
        P("spec", None, "lon"),
        P(None, "spec", None, "lon"),
        P(),
        P(),
        P(),
        P(None, "lon"),
        P(None, None, "lon"),
        P(None, None, "lon"),
    )
    out_specs = P("spec", None, "lon")
    return jax.shard_map(
        functools.partial(per_device, mesh.shape["spec"], mesh.shape["lon"]),
        mesh=mesh, in_specs=in_specs, out_specs=out_specs, check_vma=False,
    )
```

time: 741 us -> 541 us (0.73)
  Pallas kernels: 0 us -> 492 us
  blocking collectives: 365 us -> 0 us
  waiting for transfers between devices: 101 us -> 0 us
  local copies, waits for them, and re-layouts: 138 us -> 40.3 us
  other arithmetic: 95.9 us -> 3.92 us
  matrix products: 18.7 us -> 0 us
  starting transfers between devices: 12.6 us -> 0 us
    pallas_call x0 -> x1, Pallas kernels: none -> 492 us  [per_device(): pl.pallas_call(functools.partial(kernel, steps, parts, ring, bounds, own_...]
    all_to_all x3 -> x0, blocking collectives: 365 us -> none  [the longest x2 245 us: per_device(): lax.all_to_all(rounded, 'spec', split_axis=1, concat_axis=0, tiled=True)]
    all_to_all x1 -> x0, waiting for transfers between devices: 101 us -> none  [per_device(): lax.all_to_all(coupled, 'spec', split_axis=0, concat_axis=1, tiled=True)]
    slice x9 -> x2, local copies, waits for them, and re-layouts: 86.8 us -> 4.01 us  [arrange_weights(): table[:, low:high]]
    add x4 -> x0, other arithmetic: 52 us -> none  [the longest x1 29.9 us: advect_step(): result + jnp.maximum(speed_y, 0.0) * northern]
    convert_element_type x3 -> x0, other arithmetic: 43.1 us -> none  [the longest x2 42.3 us: per_device(): rounded = adjoint.astype(jnp.bfloat16)]
    reshape x0 -> x6, local copies, waits for them, and re-layouts: none -> 24.8 us  [the longest x2 18 us: arrange_weights(): table = mixing.T.reshape(parts, own, parts, own)]
    ppermute x4 -> x0, local copies, waits for them, and re-layouts: 22.4 us -> none  [the longest x2 11.2 us: with_halo(): lax.ppermute(lax.slice_in_dim(block, block.shape[dim] - width, None, axis...]
  transfers between devices with their start and end apart: 5 -> 0, of which waited for: 1 -> 0; matrix products, arithmetic and copies ran while one was open for 7% -> 0% of each run, Pallas kernels for 0% -> 0%
where the time goes in v1:
time: 541 us; the launch traced here: 536 us
  Pallas kernels  492 us (91%)
  local copies, waits for them, and re-layouts  40.3 us (7%)
    pallas_call x1, Pallas kernels, per_device(): pl.pallas_call(functools.partial(kernel, steps, parts, ring, bounds, own_...  492 us
    reshape x2, local copies, waits for them, and re-layouts, arrange_weights(): table = mixing.T.reshape(parts, own, parts, own)  18 us
    unnamed x5, local copies, waits for them, and re-layouts  11 us

profile of v1, /device:TPU:8, one launch (start us, length us, event | category | flops | bytes accessed | tf_op | source)
XLA Modules:
  0.0 536.3 jit_solution(9693054526193209763)
XLA Ops:
  0.0 9.2 %reshape.15 = bf16[4,324,4,324]{1,0,3,2:T(4,128)(2,1)} reshape(bf16[1296,1296]{0,1:T(8,128)(2,1)} %bitcast.3) | data formatting | bytes 6718464 | tf_op jit(solution)/shard_map/reshape | solution.py:300
  9.2 8.8 %copy.9 = bf16[4,324,4,324]{3,2,1,0:T(4,128)(2,1)} copy(bf16[4,324,4,324]{1,0,3,2:T(4,128)(2,1)} %reshape.15) | data formatting | bytes 6718464 | tf_op jit(solution)/shard_map/reshape | solution.py:300
  18.0 0.0 copy-start
  18.0 1.9 pad_slice_fusion
  19.9 0.6 copy-done
  20.5 2.1 pad_slice_fusion.3
  22.6 1.6 reshape.16
  24.2 0.4 pad.9
  24.7 0.8 reshape.19
  25.5 0.0 copy-start.1
  25.5 2.8 reshape.17
  28.3 1.6 reshape.18
  29.9 0.0 copy-done.1
  29.9 3.9 pad_maximum_fusion.weights
  33.8 492.1 %shard_map.82 = f32[324,64,128]{2,1,0:T(8,128)} custom-call(f32[324,64,128]{2,1,0:T(8,128)} %lam.1, bf16[2,324,64,128]{3,2,1,0:T(8,128)(2,1)} %source.1, bf16[1312,1344]{1,0:T(8,128)(2,1)} %pad_maximum_fusion.weights, f32[1296]{0:T(1024)} %drift_x.1, f32[1296]{0:T(1024)} %drift_y.1, s32[64,128]{1,0:T(8,128)} %ocean_mask.1, f32[2,64,128]{2,1,0:T(8,128)} %misfit.1, ...), custom_call_target="tpu_custom_call" | custom-call | tf_op jit(solution)/shard_map/pallas_call | solution.py:326
  525.9 10.4 %copy.11 = f32[324,64,128]{2,1,0:T(8,128)} copy(f32[324,64,128]{2,1,0:T(8,128)} %shard_map.82) | data formatting | bytes 21233664
Async XLA Ops:
  18.0 2.4 copy-start
  25.5 4.4 copy-start.1

commit v2 on v1

--- a/solution.py
+++ b/solution.py
@@ -27,9 +27,9 @@
 
 def kernel(
     steps, parts, ring, bounds, own_pad,
-    lam, source, weights, drift_x, drift_y, ocean_mask, misfit, obs_mask,
+    lam, source, mixing, drift_x, drift_y, ocean_mask, misfit, obs_mask,
     out,
-    state, send_in, recv_in, send_out, recv_out, flat, weight_buf, spread, unpack,
+    state, send_in, recv_in, send_out, recv_out, flat, mixing_buf, arranged, weight_buf, spread, unpack,
     source_buf, halo_send, halo_recv,
     send_sem, recv_sem, halo_send_sem, halo_recv_sem, lam_sem, source_sem, weight_sem, out_sem,
 ):
@@ -39,11 +39,14 @@
     rows = lat // parts
     east, west = lax.rem(lon + 1, ring), lax.rem(lon + ring - 1, ring)
     chunks = len(bounds)
-    peers = list(range(1, parts))
+    peers = list(range(parts - 1))
+    half = max(parts // 2, 1)
     order = [(step, q) for step in reversed(range(steps)) for q in range(chunks)]
 
-    def peer(offset):
-        return lax.rem(me + offset, parts)
+    def peer(index):
+        if index < half:
+            return half - lax.div(me, half) * half + lax.rem(me + index, half)
+        return lax.div(me, half) * half + lax.rem(me + index - half + 1, half)
 
     def lam_copy(q):
         low, high = bounds[q]
@@ -67,7 +70,7 @@
             state.at[pl.ds(low, high - low)], out.at[pl.ds(low, high - low)], out_sem.at[q]
         )
 
-    weight_copy = pltpu.make_async_copy(weights, weight_buf, weight_sem)
+    mixing_copy = pltpu.make_async_copy(mixing, mixing_buf, weight_sem)
 
     def exchange(phase, q, offset):
         low, high = bounds[q]
@@ -76,7 +79,7 @@
         return pltpu.make_async_remote_copy(
             src_ref=sender.at[target, pl.ds(low, high - low)],
             dst_ref=receiver.at[me, pl.ds(low, high - low)],
-            send_sem=send_sem.at[phase, q, offset - 1],
+            send_sem=send_sem.at[phase, q, offset],
             recv_sem=recv_sem.at[phase, q, me],
             device_id={"spec": target},
             device_id_type=MESH,
@@ -89,7 +92,7 @@
         return pltpu.make_async_remote_copy(
             src_ref=sender.at[origin, pl.ds(low, high - low)],
             dst_ref=receiver.at[origin, pl.ds(low, high - low)],
-            send_sem=send_sem.at[phase, q, offset - 1],
+            send_sem=send_sem.at[phase, q, offset],
             recv_sem=recv_sem.at[phase, q, origin],
             device_id={"spec": origin},
             device_id_type=MESH,
@@ -107,7 +110,7 @@
 
     for q in range(chunks):
         lam_copy(q).start()
-    weight_copy.start()
+    mixing_copy.start()
     source_copy(0).start()
     source_copy(1).start()
 
@@ -144,6 +147,51 @@
         for offset in peers:
             exchange(0, q, offset).start()
 
+    mixing_copy.wait()
+    components = parts * own
+    start = 0
+    for q in range(chunks):
+        low, high = bounds[q]
+        tall = round_up(high - low, 16)
+        piece_row = lax.broadcasted_iota(jnp.int32, (tall, components), 0)
+        piece_column = lax.broadcasted_iota(jnp.int32, (tall, components), 1)
+
+        def arrange(part, carry):
+            wanted = (piece_column == part * own + low + piece_row) & (piece_row < high - low)
+            arranged[pl.ds(pl.multiple_of(start + part * tall, 16), tall)] = lax.dot_general(
+                wanted.astype(jnp.float32).astype(jnp.bfloat16),
+                mixing_buf[...],
+                (((1,), (1,)), ((), ())),
+                preferred_element_type=jnp.float32,
+            ).astype(jnp.bfloat16)
+            return carry
+
+        lax.fori_loop(0, parts, arrange, 0)
+        start += parts * tall
+
+    def spread_columns(origin, carry):
+        pick_row = lax.broadcasted_iota(jnp.int32, (components, own_pad), 0)
+        pick_column = lax.broadcasted_iota(jnp.int32, (components, own_pad), 1)
+        pick = (pick_row == origin * own + pick_column) & (pick_column < own)
+        mixing_buf[:, :own_pad] = pick.astype(jnp.float32).astype(jnp.bfloat16)
+        block = weight_buf.shape[0] // 4
+
+        def rows_of(t, inner):
+            place = pl.ds(pl.multiple_of(t * block, 16), block)
+            weight_buf[place, pl.ds(pl.multiple_of(origin * own_pad, 128), own_pad)] = jnp.dot(
+                arranged[place], mixing_buf[:, :own_pad], preferred_element_type=jnp.float32
+            ).astype(jnp.bfloat16)
+            return inner
+
+        return lax.fori_loop(0, 4, rows_of, carry)
+
+    lax.fori_loop(0, parts, spread_columns, 0)
+
+    for origin in range(parts):
+        flat[origin * own_pad + own : (origin + 1) * own_pad] = jnp.zeros(
+            (own_pad - own, rows * width), jnp.bfloat16
+        )
+
     for step in reversed(range(steps)):
         last = step == 0
 
@@ -153,11 +201,12 @@
             padded = round_up(count, 16)
             group = group_of(count)
 
-            for offset in range(parts):
-                origin = peer(offset)
-                if offset:
+            for offset in [None] + peers:
+                if offset is None:
+                    origin, block = me, send_in
+                else:
+                    origin, block = peer(offset), recv_in
                     arrival(0, q, offset).wait_recv()
-                block = recv_in if offset else send_in
                 if padded != count:
                     unpack[pl.ds(count * rows, (padded - count) * rows)] = jnp.zeros(
                         ((padded - count) * rows, width), jnp.float32
@@ -177,13 +226,11 @@
                         pl.ds(i, padded, stride=rows)
                     ].astype(jnp.bfloat16)
 
-        if step == steps - 1:
-            weight_copy.wait()
         start = 0
         for q in range(chunks):
             low, high = bounds[q]
             count = high - low
-            tall = round_up(count, 8)
+            tall = round_up(count, 16)
             group = group_of(count)
             total = parts * tall
 
@@ -296,17 +343,6 @@
         out_copy(q).wait()
 
 
-def arrange_weights(mixing, parts, own, own_pad, bounds):
-    table = mixing.T.reshape(parts, own, parts, own)
-    table = jnp.pad(table, ((0, 0), (0, 0), (0, 0), (0, own_pad - own)))
-    pieces = []
-    for low, high in bounds:
-        tall = round_up(high - low, 8)
-        piece = jnp.pad(table[:, low:high], ((0, 0), (0, tall - (high - low)), (0, 0), (0, 0)))
-        pieces.append(piece.reshape(parts * tall, parts * own_pad))
-    return jnp.concatenate(pieces, axis=0)
-
-
 def per_device(
     parts, ring, lam_final, stored_source, mixing, drift_x, drift_y, ocean_mask, misfit, obs_mask
 ):
@@ -314,9 +350,9 @@
     own, lat, width = lam_final.shape
     rows = lat // parts
     bounds = chunk_bounds(own)
-    own_pad = round_up(own, 16)
+    own_pad = round_up(own, 128)
     largest = max(high - low for low, high in bounds)
-    weights = arrange_weights(mixing, parts, own, own_pad, bounds)
+    tall = sum(round_up(high - low, 16) for low, high in bounds) * parts
     vmem = pl.BlockSpec(memory_space=pltpu.VMEM)
     smem = pl.BlockSpec(memory_space=pltpu.SMEM)
     hbm = pl.BlockSpec(memory_space=pl.ANY)
@@ -332,8 +368,10 @@
             pltpu.VMEM((own, lat, width), jnp.float32),
             block, block, block, block,
             pltpu.VMEM((parts * own_pad, rows * width), jnp.bfloat16),
-            pltpu.VMEM(weights.shape, jnp.bfloat16),
-            pltpu.VMEM((parts * round_up(largest, 8) * rows, width), jnp.float32),
+            pltpu.VMEM(mixing.shape, jnp.bfloat16),
+            pltpu.VMEM((tall, parts * own), jnp.bfloat16),
+            pltpu.VMEM((tall, parts * own_pad), jnp.bfloat16),
+            pltpu.VMEM((parts * round_up(largest, 16) * rows, width), jnp.float32),
             pltpu.VMEM((round_up(largest, 16) * rows, width), jnp.float32),
             pltpu.VMEM((2, largest, lat, width), jnp.bfloat16),
             pltpu.VMEM((positions, 2, lat, width), jnp.float32),
@@ -350,7 +388,7 @@
         compiler_params=pltpu.CompilerParams(
             collective_id=0, has_side_effects=True, vmem_limit_bytes=60 * 1024 * 1024
         ),
-    )(lam_final, stored_source, weights, drift_x, drift_y, ocean_mask, misfit, obs_mask)
+    )(lam_final, stored_source, mixing, drift_x, drift_y, ocean_mask, misfit, obs_mask)
 
 
 def solution(mesh):

time: 541 us -> 501 us (0.926)
  local copies, waits for them, and re-layouts: 40.3 us -> 10.4 us
    reshape x6 -> x0, local copies, waits for them, and re-layouts: 24.8 us -> none  [the longest x2 18 us: arrange_weights(): table = mixing.T.reshape(parts, own, parts, own)]
    unnamed x5 -> x1, local copies, waits for them, and re-layouts: 11 us -> 10.4 us
where the time goes in v2:
time: 501 us
  Pallas kernels  491 us (98%)
  local copies, waits for them, and re-layouts  10.4 us (2%)
    pallas_call x1, Pallas kernels, per_device(): pl.pallas_call(functools.partial(kernel, steps, parts, ring, bounds, own_...  491 us
    unnamed x1, local copies, waits for them, and re-layouts  10.4 us

profile of v2, /device:TPU:8, one launch (start us, length us, event | category | flops | bytes accessed | tf_op | source)
XLA Modules:
  0.0 501.2 jit_solution(10903188483158139555)
XLA Ops:
  0.0 490.8 %shard_map.82 = f32[324,64,128]{2,1,0:T(8,128)} custom-call(f32[324,64,128]{2,1,0:T(8,128)} %lam.1, bf16[2,324,64,128]{3,2,1,0:T(8,128)(2,1)} %source.1, bf16[1296,1296]{1,0:T(8,128)(2,1)} %mixing.1, f32[1296]{0:T(1024)} %drift_x.1, f32[1296]{0:T(1024)} %drift_y.1, s32[64,128]{1,0:T(8,128)} %ocean_mask.1, f32[2,64,128]{2,1,0:T(8,128)} %misfit.1, ...), custom_call_target="tpu_custom_call" | custom-call | tf_op jit(solution)/shard_map/pallas_call | solution.py:362
  490.8 10.4 %copy.10 = f32[324,64,128]{2,1,0:T(8,128)} copy(f32[324,64,128]{2,1,0:T(8,128)} %shard_map.82) | data formatting | bytes 21233664

commit v3 on v2

--- a/solution.py
+++ b/solution.py
@@ -7,12 +7,13 @@
 from jax.experimental.pallas import tpu as pltpu
 from jax.sharding import PartitionSpec as P
 
-CHUNKS = 4
+SHARES = (0.15, 0.5, 0.85)
+CHUNKS = len(SHARES) + 1
 MESH = pl.DeviceIdType.MESH
 
 
 def chunk_bounds(own):
-    inner = [int(round(own * q / CHUNKS / 16)) * 16 for q in range(1, CHUNKS)]
+    inner = [int(round(own * share / 16)) * 16 for share in SHARES]
     edges = [0] + inner + [own]
     return list(zip(edges[:-1], edges[1:]))
 
@@ -249,20 +250,21 @@
             if not step == steps - 1:
                 for offset in peers:
                     exchange(1, q, offset).wait_send()
-            for part in range(parts):
+            for offset in peers + [None]:
+                part = me if offset is None else peer(offset)
+                target = recv_out if offset is None else send_out
 
                 def narrow(t, carry):
                     place = pl.multiple_of((part * tall + t * group) * rows, 8)
                     value = spread[pl.ds(place, group * rows)]
-                    send_out[part, pl.ds(low + t * group, group)] = value.reshape(
+                    target[part, pl.ds(low + t * group, group)] = value.reshape(
                         group, rows, width
                     ).astype(jnp.bfloat16)
                     return carry
 
                 lax.fori_loop(0, count // group, narrow, 0)
-            for offset in peers:
-                exchange(1, q, offset).start()
-            recv_out[me, pl.ds(low, count)] = send_out[me, pl.ds(low, count)]
+                if offset is not None:
+                    exchange(1, q, offset).start()
             start += total
 
         forcing = None if last else forcing_of(step - 1)

time: 501 us -> 509 us (1.016)
  Pallas kernels: 491 us -> 498 us
    pallas_call x1, Pallas kernels: 491 us -> 498 us  [per_device(): pl.pallas_call(functools.partial(kernel, steps, parts, ring, bounds, own_...]
where the time goes in v3:
time: 509 us; the launch traced here: 508 us
  Pallas kernels  498 us (98%)
  local copies, waits for them, and re-layouts  10.4 us (2%)
    pallas_call x1, Pallas kernels, per_device(): pl.pallas_call(functools.partial(kernel, steps, parts, ring, bounds, own_...  498 us
    unnamed x1, local copies, waits for them, and re-layouts  10.4 us

profile of v3, /device:TPU:8, one launch (start us, length us, event | category | flops | bytes accessed | tf_op | source)
XLA Modules:
  0.0 508.4 jit_solution(2386683679363344787)
XLA Ops:
  0.0 498.0 %shard_map.82 = f32[324,64,128]{2,1,0:T(8,128)} custom-call(f32[324,64,128]{2,1,0:T(8,128)} %lam.1, bf16[2,324,64,128]{3,2,1,0:T(8,128)(2,1)} %source.1, bf16[1296,1296]{1,0:T(8,128)(2,1)} %mixing.1, f32[1296]{0:T(1024)} %drift_x.1, f32[1296]{0:T(1024)} %drift_y.1, s32[64,128]{1,0:T(8,128)} %ocean_mask.1, f32[2,64,128]{2,1,0:T(8,128)} %misfit.1, ...), custom_call_target="tpu_custom_call" | custom-call | tf_op jit(solution)/shard_map/pallas_call | solution.py:364
  498.0 10.4 %copy.10 = f32[324,64,128]{2,1,0:T(8,128)} copy(f32[324,64,128]{2,1,0:T(8,128)} %shard_map.82) | data formatting | bytes 21233664
